TPU v7x, 256 devices: a whole 4x4x8 slice. The times are simulated.
256 devices in a mesh: train: 16 (over z, core), query: 16 (over y, x).
Axes of the slice: x: 4, y: 4, z: 8, core: 2. Of those that a mesh axis runs over, the one named last changes fastest.
Arguments:
- train_hidden: bfloat16 [512, 96, 4096], P(('train', 'query')), may hold values from -6 to 6
- train_outgrad: bfloat16 [512, 96, 14336], P(('train', 'query')), may hold values from -6 to 6
- train_mask: int32 [512, 96], P(('train', 'query')), may hold values 0 or 1
- query_hidden: bfloat16 [256, 96, 4096], P(('train', 'query')), may hold values from -6 to 6
- query_outgrad: bfloat16 [256, 96, 14336], P(('train', 'query')), may hold values from -6 to 6
- query_mask: int32 [256, 96], P(('train', 'query')), may hold values 0 or 1
- proj_in: bfloat16 [4096, 64], replicated, may hold values from -0.09375 to 0.09375
- proj_out: bfloat16 [14336, 64], replicated, may hold values from -0.046875 to 0.046875
Outputs:
- scores: float32 [512, 256], P(('train', 'query'))
All inputs are finite; a program needn't handle non-finite values. No bound on the sum of `train_mask` or of `query_mask` on one device may be relied on, other than what follows from the above.
Results may differ from a plain program's by a relative error of at most 0.0003.
Values sent between devices are 32-bit elements; how exact they have to be, the bound alone decides.
A program may use at most 128 MiB of HBM per device.

v0:
```python
import jax
import jax.numpy as jnp
from jax import lax
from jax.sharding import PartitionSpec as P

damping_share = 0.1
AXES = ("train", "query")
HIGHEST = lax.Precision.HIGHEST


def sketch_terms(hidden, outgrad, mask, proj_in, proj_out):
    proof_count, token_count, model_width = hidden.shape
    input_side = jnp.dot(
        hidden.reshape(proof_count * token_count, model_width),
        proj_in,
        preferred_element_type=jnp.float32,
    )
    output_side = jnp.dot(
        outgrad.reshape(proof_count * token_count, -1), proj_out, preferred_element_type=jnp.float32
    )
    output_side = output_side * mask.reshape(-1, 1).astype(jnp.float32)
    input_side = input_side.reshape(proof_count, token_count, -1)
    output_side = output_side.reshape(proof_count, token_count, -1)
    outer_sum = jnp.einsum("pti,ptj->pij", output_side, input_side, precision=HIGHEST)
    return outer_sum.reshape(proof_count, -1)


def spd_solve(system, right, tolerance=0.001, most_steps=48):
    size = system.shape[0]
    eye = jnp.eye(size, dtype=system.dtype)
    diagonal = jnp.sum(system * eye, axis=1)
    inv_sqrt = lax.rsqrt(diagonal)
    bound = jnp.max(jnp.sum(jnp.abs(system) * inv_sqrt[:, None] * inv_sqrt[None, :], axis=1))
    start = eye * (1.0 / (diagonal * bound))[None, :]

    def going(carry):
        step, _, residual = carry
        return (step < most_steps) & (residual > tolerance)

    def one_step(inverse):
        remainder = eye - jnp.dot(system, inverse, precision=HIGHEST)
        residual = jnp.sqrt(jnp.sum(remainder * remainder))
        return (inverse + jnp.dot(inverse, remainder, precision=HIGHEST), residual)

    def advance(carry):
        step, inverse, _ = carry
        for _ in range(3):
            inverse, _ = one_step(inverse)
        inverse, residual = one_step(inverse)
        return (step + 4, inverse, residual)

    _, inverse, _ = lax.while_loop(
        going, advance, (jnp.int32(0), start, jnp.array(jnp.inf, system.dtype))
    )
    solved = jnp.dot(inverse, right, precision=HIGHEST)
    return solved + jnp.dot(
        inverse, right - jnp.dot(system, solved, precision=HIGHEST), precision=HIGHEST
    )


def body(
    train_hidden,
    train_outgrad,
    train_mask,
    query_hidden,
    query_outgrad,
    query_mask,
    proj_in,
    proj_out,
):
    train_sketch = sketch_terms(train_hidden, train_outgrad, train_mask, proj_in, proj_out)
    query_sketch = sketch_terms(query_hidden, query_outgrad, query_mask, proj_in, proj_out)
    block_rows = train_sketch.shape[0]
    width = train_sketch.shape[1]
    both = jnp.concatenate([train_sketch, query_sketch], axis=0)
    within = lax.all_gather(both.reshape(1, -1), AXES[1], axis=0, tiled=True)
    everyone = lax.all_gather(within, AXES[0], axis=0, tiled=True)
    devices = everyone.shape[0]
    pieces = [everyone[:, r * width : (r + 1) * width] for r in range(block_rows + 1)]
    all_train = jnp.concatenate(pieces[:block_rows], axis=0)
    gram_matrix = jnp.dot(all_train, all_train.T, precision=HIGHEST)
    products = jnp.dot(all_train, pieces[block_rows].T, precision=HIGHEST)
    total_rows = gram_matrix.shape[0]
    eye = jnp.eye(total_rows, dtype=jnp.float32)
    damping = damping_share * jnp.sum(gram_matrix * eye) / total_rows
    system = gram_matrix + damping * eye
    system, products = lax.optimization_barrier((system, products))
    solved = total_rows * spd_solve(system, products)
    me = lax.axis_index(AXES)
    return jnp.concatenate(
        [lax.dynamic_slice_in_dim(solved, r * devices + me, 1, 0) for r in range(block_rows)],
        axis=0,
    )


def solution(mesh):
    in_specs = (
        P(AXES, None, None),
        P(AXES, None, None),
        P(AXES, None),
        P(AXES, None, None),
        P(AXES, None, None),
        P(AXES, None),
        P(),
        P(),
    )
    out_specs = P(AXES, None)
    return jax.shard_map(body, mesh=mesh, in_specs=in_specs, out_specs=out_specs, check_vma=False)
```

profile of v0, /device:TPU:1, one launch (start us, length us, event | category | flops | bytes accessed | tf_op | source)
XLA Modules:
  0.0 246.9 jit_solution(12028360750653401418)
XLA Ops:
  9.8 2.4 fusion.9
  12.5 5.1 %convolution_multiply_fusion = f32[192,64]{0,1:T(8,128)S(1)} fusion(bf16[192,14336]{1,0:T(8,128)(2,1)} %bitcast.103, bf16[14336,64]{0,1:T(8,128)(2,1)} %param.17, f32[192]{0:T(256)S(1)} %convert_element_type.33), kind=kOutput, calls=%fused_computation.24 | convolution fusion | flops 352333824 | bytes 7389952 | tf_op jit(solution)/shard_map/dot_general | solution.py:18
  17.7 2.1 fusion.15
  20.2 20.5 %all-gather = f32[16,1,12288]{2,1,0:T(1,128)S(1)} all-gather(f32[1,1,12288]{2,1,0:T(1,128)S(1)} %reshape.68), channel_id=1, replica_groups=mesh['train'=16,'query'=16] {'query'}, dimensions={0}, use_global_device_ids=true | all-gather | bytes 835584 | tf_op jit(solution)/shard_map/all_gather | solution.py:76
  42.1 82.2 %all-gather.3.cloned.1.call-done = f32[256,12288]{1,0:T(8,128)} async-done(((f32[16,12288]{1,0:T(8,128)}), f32[256,12288]{1,0:T(8,128)}) %all-gather.3.cloned.1.call-update) | async-done | bytes 12582928 | tf_op jit(solution)/shard_map/all_gather | solution.py:77
  124.3 4.0 %fusion.21 = (f32[256,4096]{1,0:T(8,128)S(1)}, f32[256,4096]{1,0:T(8,128)S(1)}) fusion(f32[256,12288]{1,0:T(8,128)} %all-gather.3.cloned.1.call-done), kind=kLoop, calls=%fused_computation.47 | loop fusion | bytes 16777216 | tf_op jit(solution)/shard_map/slice | solution.py:79
  128.4 15.9 %select_reduce_fusion.1 = (f32[]{:T(128)}, f32[512,512]{1,0:T(8,128)}) fusion(f32[256,4096]{1,0:T(8,128)S(1)} %get-tuple-element.91, f32[256,4096]{1,0:T(8,128)S(1)} %get-tuple-element.90), kind=kOutput, calls=%fused_computation.29 | convolution fusion | flops 12887785472 | bytes 9437188 | tf_op jit(solution)/shard_map/dot_general | solution.py:81
  146.3 10.6 %fusion.3 = f32[512,256]{1,0:T(8,128)S(1)} fusion(f32[256,4096]{1,0:T(8,128)} %copy-done.6, f32[256,4096]{1,0:T(8,128)} %copy-done.5, f32[256,12288]{1,0:T(8,128)} %all-gather.3.cloned.1.call-done), kind=kOutput, calls=%fused_computation.16 | convolution fusion | flops 6444548096 | bytes 13107200 | tf_op jit(solution)/shard_map/dot_general | solution.py:82
  159.7 2.5 %copy.18 = f32[512,512]{0,1:T(8,128)} copy(f32[512,512]{1,0:T(8,128)} %fusion.12) | data formatting | bytes 2097152
  162.3 70.0 %while.14 = (s32[]{:T(128)}, f32[512,512]{0,1:T(8,128)}, f32[]{:T(128)}, f32[512,512]{1,0:T(8,128)}, s32[]{:T(128)}) while((s32[]{:T(128)}, f32[512,512]{0,1:T(8,128)}, f32[]{:T(128)}, f32[512,512]{1,0:T(8,128)}, s32[]{:T(128)}) %tuple.39), condition=%wide.region_6.0_spmd.clone.clone, body=%wide.region_4.0_spmd.clone.clone.sunk | while | flops 12889620480 | bytes 33554572 | solution.py:52
  162.3 3.5 %convert_subtract_fusion.7 = f32[512,512]{0,1:T(8,128)S(1)} fusion(f32[512,512]{1,0:T(8,128)} %get-tuple-element.137, f32[512,512]{0,1:T(8,128)} %get-tuple-element.130), kind=kOutput, calls=%fused_computation.4.clone.1 | convolution fusion | flops 1611399168 | bytes 3145728 | tf_op jit(solution)/shard_map/while/body/dot_general | solution.py:41
  165.8 3.4 %fusion.87 = f32[512,512]{0,1:T(8,128)S(1)} fusion(f32[512,512]{0,1:T(8,128)} %get-tuple-element.130, f32[512,512]{0,1:T(8,128)S(1)} %convert_subtract_fusion.7), kind=kOutput, calls=%fused_computation.12.clone.1 | convolution fusion | flops 1610874880 | bytes 3145728 | tf_op jit(solution)/shard_map/while/body/dot_general | solution.py:43
  171.1 1.9 convolution_add_fusion.7
  173.0 1.9 convert_subtract_fusion.9
  174.8 1.9 convolution_add_fusion.8
  176.7 3.5 %multiply_reduce_fusion.3 = (f32[]{:T(128)}, f32[512,512]{0,1:T(8,128)}) fusion(f32[512,512]{0,1:T(8,128)S(1)} %convolution_add_fusion.8, f32[512,512]{1,0:T(8,128)S(1)} %copy-done.2), kind=kOutput, calls=%fused_computation.14.clone.1 | convolution fusion | flops 1611923456 | bytes 3145732 | tf_op jit(solution)/shard_map/while/body/dot_general | solution.py:41
  180.9 4.7 %convolution_add_fusion.9 = f32[512,512]{0,1:T(8,128)} fusion(f32[512,512]{0,1:T(8,128)} %copy-done.3, f32[512,512]{0,1:T(8,128)} %get-tuple-element.122), kind=kOutput, calls=%fused_computation.5.clone.1 | convolution fusion | flops 1610874880 | bytes 3145728 | tf_op jit(solution)/shard_map/while/body/dot_general | solution.py:43
  185.6 3.5 %convert_subtract_fusion.7 = f32[512,512]{0,1:T(8,128)S(1)} fusion(f32[512,512]{1,0:T(8,128)} %get-tuple-element.137, f32[512,512]{0,1:T(8,128)} %get-tuple-element.130), kind=kOutput, calls=%fused_computation.4.clone.1 | convolution fusion | flops 1611399168 | bytes 3145728 | tf_op jit(solution)/shard_map/while/body/dot_general | solution.py:41
  189.1 3.4 %fusion.87 = f32[512,512]{0,1:T(8,128)S(1)} fusion(f32[512,512]{0,1:T(8,128)} %get-tuple-element.130, f32[512,512]{0,1:T(8,128)S(1)} %convert_subtract_fusion.7), kind=kOutput, calls=%fused_computation.12.clone.1 | convolution fusion | flops 1610874880 | bytes 3145728 | tf_op jit(solution)/shard_map/while/body/dot_general | solution.py:43
  194.4 1.9 convolution_add_fusion.7
  196.3 1.9 convert_subtract_fusion.9
  198.2 1.9 convolution_add_fusion.8
  200.1 3.5 %multiply_reduce_fusion.3 = (f32[]{:T(128)}, f32[512,512]{0,1:T(8,128)}) fusion(f32[512,512]{0,1:T(8,128)S(1)} %convolution_add_fusion.8, f32[512,512]{1,0:T(8,128)S(1)} %copy-done.2), kind=kOutput, calls=%fused_computation.14.clone.1 | convolution fusion | flops 1611923456 | bytes 3145732 | tf_op jit(solution)/shard_map/while/body/dot_general | solution.py:41
  204.2 4.7 %convolution_add_fusion.9 = f32[512,512]{0,1:T(8,128)} fusion(f32[512,512]{0,1:T(8,128)} %copy-done.3, f32[512,512]{0,1:T(8,128)} %get-tuple-element.122), kind=kOutput, calls=%fused_computation.5.clone.1 | convolution fusion | flops 1610874880 | bytes 3145728 | tf_op jit(solution)/shard_map/while/body/dot_general | solution.py:43
  208.9 3.5 %convert_subtract_fusion.7 = f32[512,512]{0,1:T(8,128)S(1)} fusion(f32[512,512]{1,0:T(8,128)} %get-tuple-element.137, f32[512,512]{0,1:T(8,128)} %get-tuple-element.130), kind=kOutput, calls=%fused_computation.4.clone.1 | convolution fusion | flops 1611399168 | bytes 3145728 | tf_op jit(solution)/shard_map/while/body/dot_general | solution.py:41
  212.4 3.4 %fusion.87 = f32[512,512]{0,1:T(8,128)S(1)} fusion(f32[512,512]{0,1:T(8,128)} %get-tuple-element.130, f32[512,512]{0,1:T(8,128)S(1)} %convert_subtract_fusion.7), kind=kOutput, calls=%fused_computation.12.clone.1 | convolution fusion | flops 1610874880 | bytes 3145728 | tf_op jit(solution)/shard_map/while/body/dot_general | solution.py:43
  217.7 1.9 convolution_add_fusion.7
  221.5 1.9 convolution_add_fusion.8
  223.4 3.5 %multiply_reduce_fusion.3 = (f32[]{:T(128)}, f32[512,512]{0,1:T(8,128)}) fusion(f32[512,512]{0,1:T(8,128)S(1)} %convolution_add_fusion.8, f32[512,512]{1,0:T(8,128)S(1)} %copy-done.2), kind=kOutput, calls=%fused_computation.14.clone.1 | convolution fusion | flops 1611923456 | bytes 3145732 | tf_op jit(solution)/shard_map/while/body/dot_general | solution.py:41
  227.5 4.7 %convolution_add_fusion.9 = f32[512,512]{0,1:T(8,128)} fusion(f32[512,512]{0,1:T(8,128)} %copy-done.3, f32[512,512]{0,1:T(8,128)} %get-tuple-element.122), kind=kOutput, calls=%fused_computation.5.clone.1 | convolution fusion | flops 1610874880 | bytes 3145728 | tf_op jit(solution)/shard_map/while/body/dot_general | solution.py:43
  232.3 3.1 %fusion.23 = f32[512,256]{1,0:T(8,128)S(1)} fusion(f32[512,512]{0,1:T(8,128)} %get-tuple-element.44, f32[512,256]{1,0:T(8,128)S(1)} %fusion.3), kind=kOutput, calls=%fused_computation.49 | convolution fusion | flops 805306368 | bytes 2097152 | tf_op jit(solution)/shard_map/dot_general | solution.py:55
  235.4 2.2 convolution_subtract_fusion
  (52 shorter events, 19.6 us)
Async XLA Ops:
  6.5 3.2 %copy-start = (bf16[1,96,14336]{2,1,0:T(8,128)(2,1)S(1)}, bf16[1,96,14336]{2,1,0:T(8,128)(2,1)}, u32[]{:S(2)}) copy-start(bf16[1,96,14336]{2,1,0:T(8,128)(2,1)} %param.14) | copy-start | bytes 8257540
  6.5 117.8 %all-gather.3.cloned.1.call-start = ((), (), s32[]{:S(2)}) async-start(), calls=%async_computation | async-start | bytes 13369344 | tf_op jit(solution)/shard_map/all_gather | solution.py:77
  12.5 5.2 %copy-start.7 = (bf16[4096,64]{0,1:T(8,128)(2,1)S(1)}, bf16[4096,64]{0,1:T(8,128)(2,1)}, u32[]{:S(2)}) copy-start(bf16[4096,64]{0,1:T(8,128)(2,1)} %param.16) | copy-start | bytes 1572868
  128.3 15.9 %copy-start.5 = (f32[256,4096]{1,0:T(8,128)}, f32[256,4096]{1,0:T(8,128)S(1)}, u32[]{:S(2)}) copy-start(f32[256,4096]{1,0:T(8,128)S(1)} %get-tuple-element.90) | copy-start | bytes 12582916
  128.4 15.9 %copy-start.6 = (f32[256,4096]{1,0:T(8,128)}, f32[256,4096]{1,0:T(8,128)S(1)}, u32[]{:S(2)}) copy-start(f32[256,4096]{1,0:T(8,128)S(1)} %get-tuple-element.91) | copy-start | bytes 12582916
  146.3 10.7 %copy-start.1 = (f32[512,512]{1,0:T(8,128)}, f32[512,512]{1,0:T(8,128)S(1)}, u32[]{:S(2)}) copy-start(f32[512,512]{1,0:T(8,128)S(1)} %select_add_fusion) | copy-start | bytes 3145732
  162.3 6.9 %copy-start.2 = (f32[512,512]{1,0:T(8,128)S(1)}, f32[512,512]{1,0:T(8,128)}, u32[]{:S(2)}) copy-start(f32[512,512]{1,0:T(8,128)} %get-tuple-element.137) | copy-start | bytes 3145732 | tf_op jit(solution)/shard_map/while
  176.7 3.5 %copy-start.3 = (f32[512,512]{0,1:T(8,128)}, f32[512,512]{0,1:T(8,128)S(1)}, u32[]{:S(2)}) copy-start(f32[512,512]{0,1:T(8,128)S(1)} %convolution_add_fusion.8) | copy-start | bytes 3145732 | tf_op jit(solution)/shard_map/while
  185.6 6.9 %copy-start.2 = (f32[512,512]{1,0:T(8,128)S(1)}, f32[512,512]{1,0:T(8,128)}, u32[]{:S(2)}) copy-start(f32[512,512]{1,0:T(8,128)} %get-tuple-element.137) | copy-start | bytes 3145732 | tf_op jit(solution)/shard_map/while
  200.0 3.5 %copy-start.3 = (f32[512,512]{0,1:T(8,128)}, f32[512,512]{0,1:T(8,128)S(1)}, u32[]{:S(2)}) copy-start(f32[512,512]{0,1:T(8,128)S(1)} %convolution_add_fusion.8) | copy-start | bytes 3145732 | tf_op jit(solution)/shard_map/while
  208.9 6.9 %copy-start.2 = (f32[512,512]{1,0:T(8,128)S(1)}, f32[512,512]{1,0:T(8,128)}, u32[]{:S(2)}) copy-start(f32[512,512]{1,0:T(8,128)} %get-tuple-element.137) | copy-start | bytes 3145732 | tf_op jit(solution)/shard_map/while
  223.4 3.5 %copy-start.3 = (f32[512,512]{0,1:T(8,128)}, f32[512,512]{0,1:T(8,128)S(1)}, u32[]{:S(2)}) copy-start(f32[512,512]{0,1:T(8,128)S(1)} %convolution_add_fusion.8) | copy-start | bytes 3145732 | tf_op jit(solution)/shard_map/while
  232.3 5.3 %copy-start.4 = (f32[512,512]{0,1:T(8,128)S(1)}, f32[512,512]{0,1:T(8,128)}, u32[]{:S(2)}) copy-start(f32[512,512]{0,1:T(8,128)} %get-tuple-element.44) | copy-start | bytes 3145732
Sparse Core Ops, SparseCore 0:
  42.2 82.0 all-gather.2
where the time goes:
time: 247 us
  matrix products  113 us (46%)
  waiting for transfers between devices  82.2 us (33%)
  blocking collectives  20.5 us (8%)
  between operations  14.3 us (6%)
  local copies, waits for them, and re-layouts  8.45 us (3%)
  other arithmetic  6.29 us (3%)
    all_gather x1, waiting for transfers between devices, body(): everyone = lax.all_gather(within, AXES[0], axis=0, tiled=True)  82.2 us
    dot_general x12, matrix products, one_step(): return (inverse + jnp.dot(inverse, remainder, precision=HIGHEST), residual)  35.7 us
    dot_general x12, matrix products, one_step(): remainder = eye - jnp.dot(system, inverse, precision=HIGHEST)  32.1 us
    all_gather x1, blocking collectives, body(): within = lax.all_gather(both.reshape(1, -1), AXES[1], axis=0, tiled=True)  20.5 us
    dot_general x1, matrix products, body(): gram_matrix = jnp.dot(all_train, all_train.T, precision=HIGHEST)  15.9 us
    dot_general x1, matrix products, body(): products = jnp.dot(all_train, pieces[block_rows].T, precision=HIGHEST)  10.6 us
    dot_general x2, matrix products, sketch_terms(): jnp.dot(outgrad.reshape(proof_count * token_count, -1), proj_out, preferr...  7.41 us
  transfers between devices with their start and end apart: 1, of which 1 were waited for; matrix products, arithmetic and copies ran while one was open for 0% of the time, Pallas kernels for 0%

commit v1 on v0

--- a/solution.py
+++ b/solution.py
@@ -74,7 +74,9 @@
     width = train_sketch.shape[1]
     both = jnp.concatenate([train_sketch, query_sketch], axis=0)
     within = lax.all_gather(both.reshape(1, -1), AXES[1], axis=0, tiled=True)
-    everyone = lax.all_gather(within, AXES[0], axis=0, tiled=True)
+    everyone = jnp.concatenate(
+        lax.all_to_all(jnp.stack([within] * lax.axis_size(AXES[0])), AXES[0], 0, 0), axis=0
+    )
     devices = everyone.shape[0]
     pieces = [everyone[:, r * width : (r + 1) * width] for r in range(block_rows + 1)]
     all_train = jnp.concatenate(pieces[:block_rows], axis=0)

time: 247 us -> 453 us (1.83); the launches traced: 247 us -> 445 us
  waiting for transfers between devices: 82.2 us -> 273 us
  starting transfers between devices: 0.01 us -> 14.3 us
  between operations: 14.3 us -> 1.01 us
  loops' own time: 2.19 us -> 12.6 us
  matrix products: 113 us -> 104 us
  local copies, waits for them, and re-layouts: 8.45 us -> 14.3 us
    all_to_all x0 -> x1, waiting for transfers between devices: none -> 273 us  [body(): lax.all_to_all(jnp.stack([within] * lax.axis_size(AXES[0])), AXES[0], 0, 0)]
    all_gather x1 -> x0, waiting for transfers between devices: 82.2 us -> none  [body(): everyone = lax.all_gather(within, AXES[0], axis=0, tiled=True)]
    all_to_all x0 -> x1, starting transfers between devices: none -> 14.3 us  [body(): lax.all_to_all(jnp.stack([within] * lax.axis_size(AXES[0])), AXES[0], 0, 0)]
    another operation x1, loops' own time: 2.19 us -> 12.6 us  [spd_solve(): lax.while_loop(going, advance, (jnp.int32(0), start, jnp.array(jnp.inf, s...]
    another operation x0 -> x1, local copies, waits for them, and re-layouts: none -> 5.89 us  [body(): jnp.stack([within] * lax.axis_size(AXES[0]))]
    dot_general x12, matrix products: 35.7 us -> 30.5 us  [one_step(): return (inverse + jnp.dot(inverse, remainder, precision=HIGHEST), residual)]
where the time goes in v1:
time: 453 us; the launch traced here: 445 us
  waiting for transfers between devices  273 us (60%)
  matrix products  104 us (23%)
  blocking collectives  20.3 us (4%)
  local copies, waits for them, and re-layouts  14.3 us (3%)
  starting transfers between devices  14.3 us (3%)
  loops' own time  12.6 us (3%)
  other arithmetic  5.72 us (1%)
    all_to_all x1, waiting for transfers between devices, body(): lax.all_to_all(jnp.stack([within] * lax.axis_size(AXES[0])), AXES[0], 0, 0)  273 us
    dot_general x12, matrix products, one_step(): return (inverse + jnp.dot(inverse, remainder, precision=HIGHEST), residual)  30.5 us
    dot_general x12, matrix products, one_step(): remainder = eye - jnp.dot(system, inverse, precision=HIGHEST)  29.4 us
    all_gather x1, blocking collectives, body(): within = lax.all_gather(both.reshape(1, -1), AXES[1], axis=0, tiled=True)  20.3 us
    dot_general x1, matrix products, body(): gram_matrix = jnp.dot(all_train, all_train.T, precision=HIGHEST)  16.3 us
    all_to_all x1, starting transfers between devices, body(): lax.all_to_all(jnp.stack([within] * lax.axis_size(AXES[0])), AXES[0], 0, 0)  14.3 us
    another operation x1, loops' own time, spd_solve(): lax.while_loop(going, advance, (jnp.int32(0), start, jnp.array(jnp.inf, s...  12.6 us
  transfers between devices with their start and end apart: 1, of which 1 were waited for; matrix products, arithmetic and copies ran while one was open for 0% of the time, Pallas kernels for 0%

profile of v1, /device:TPU:1, one launch (start us, length us, event | category | flops | bytes accessed | tf_op | source)
XLA Modules:
  0.0 445.1 jit_solution(8024454383910993749)
XLA Ops:
  0.9 5.0 %convolution_multiply_fusion = f32[192,64]{0,1:T(8,128)S(1)} fusion(bf16[192,14336]{1,0:T(8,128)(2,1)} %bitcast.104, bf16[14336,64]{0,1:T(8,128)(2,1)} %param.17, f32[192]{0:T(256)S(1)} %convert_element_type.33), kind=kOutput, calls=%fused_computation.24 | convolution fusion | flops 352333824 | bytes 7389952 | tf_op jit(solution)/shard_map/dot_general | solution.py:18
  6.1 2.1 fusion.15
  10.1 2.4 fusion.9
  12.9 20.3 %all-gather = f32[16,1,12288]{2,1,0:T(1,128)S(1)} all-gather(f32[1,1,12288]{2,1,0:T(1,128)S(1)} %reshape.74), channel_id=1, replica_groups=mesh['train'=16,'query'=16] {'query'}, dimensions={0}, use_global_device_ids=true | all-gather | bytes 835584 | tf_op jit(solution)/shard_map/all_gather | solution.py:76
  33.6 5.9 %stack.2 = f32[16,16,12288]{2,1,0:T(8,128)} broadcast(f32[16,12288]{1,0:T(8,128)S(1)} %bitcast.105), dimensions={1,2} | broadcast | bytes 13369344 | tf_op jit(solution)/shard_map/stack | solution.py:78
  39.5 14.3 %all-to-all-start = ((f32[16,16,12288]{2,1,0:T(8,128)}), f32[16,16,12288]{2,1,0:T(8,128)}, u32[]{:S(2)}, u32[]{:S(2)}) async-start(f32[16,16,12288]{2,1,0:T(8,128)} %stack.2), calls=%async_computation | async-start | bytes 25165824 | tf_op jit(solution)/shard_map/all_to_all | solution.py:78
  53.9 273.2 %all-to-all-done = f32[16,16,12288]{2,1,0:T(8,128)} async-done(((f32[16,16,12288]{2,1,0:T(8,128)}), f32[16,16,12288]{2,1,0:T(8,128)}, u32[]{:S(2)}, u32[]{:S(2)}) %all-to-all-start) | async-done | bytes 12582944 | tf_op jit(solution)/shard_map/all_to_all | solution.py:78
  327.0 4.0 fusion.21
  331.1 16.3 %select_reduce_fusion.1 = (f32[]{:T(128)}, f32[512,512]{1,0:T(8,128)}) fusion(f32[256,4096]{1,0:T(8,128)S(1)} %get-tuple-element.91, f32[256,4096]{1,0:T(8,128)S(1)} %get-tuple-element.90), kind=kOutput, calls=%fused_computation.29 | convolution fusion | flops 12887785472 | bytes 9437188 | tf_op jit(solution)/shard_map/dot_general | solution.py:83
  347.3 9.0 %fusion.3 = f32[512,256]{1,0:T(8,128)S(1)} fusion(f32[256,4096]{1,0:T(8,128)S(1)} %get-tuple-element.91, f32[256,4096]{1,0:T(8,128)S(1)} %get-tuple-element.90, f32[256,12288]{1,0:T(8,128)} %bitcast.5), kind=kOutput, calls=%fused_computation.16 | convolution fusion | flops 6444548096 | bytes 13107200 | tf_op jit(solution)/shard_map/dot_general | solution.py:84
  362.0 2.6 copy.18
  364.6 72.5 %while.14 = (s32[]{:T(128)}, f32[512,512]{0,1:T(8,128)}, f32[]{:T(128)}, f32[512,512]{1,0:T(8,128)}, s32[]{:T(128)}) while((s32[]{:T(128)}, f32[512,512]{0,1:T(8,128)}, f32[]{:T(128)}, f32[512,512]{1,0:T(8,128)}, s32[]{:T(128)}) %tuple.37), condition=%wide.region_6.0_spmd.clone.clone, body=%wide.region_4.0_spmd.clone.clone.sunk | while | flops 12889620480 | bytes 29360240 | solution.py:52
  374.8 3.5 convert_subtract_fusion.7
  378.3 3.5 fusion.87
  383.7 1.9 convolution_add_fusion.7
  387.4 1.9 convolution_add_fusion.8
  389.3 2.6 multiply_reduce_fusion.3
  391.9 2.9 convolution_add_fusion.9
  395.5 3.5 convert_subtract_fusion.7
  399.0 3.5 fusion.87
  404.4 1.9 convolution_add_fusion.7
  408.2 1.9 convolution_add_fusion.8
  410.0 2.6 multiply_reduce_fusion.3
  412.6 2.9 convolution_add_fusion.9
  416.2 3.5 convert_subtract_fusion.7
  419.7 3.5 fusion.87
  425.1 1.9 convolution_add_fusion.7
  428.9 1.9 convolution_add_fusion.8
  430.8 2.6 multiply_reduce_fusion.3
  433.4 2.9 convolution_add_fusion.9
  437.1 3.1 fusion.23
  440.3 2.2 convolution_subtract_fusion
  (44 shorter events, 22.4 us)
Async XLA Ops:
  0.0 10.0 %copy-start = (bf16[1,96,14336]{2,1,0:T(8,128)(2,1)S(1)}, bf16[1,96,14336]{2,1,0:T(8,128)(2,1)}, u32[]{:S(2)}) copy-start(bf16[1,96,14336]{2,1,0:T(8,128)(2,1)} %param.14) | copy-start | bytes 8257540
  0.9 5.2 %copy-start.4 = (bf16[4096,64]{0,1:T(8,128)(2,1)S(1)}, bf16[4096,64]{0,1:T(8,128)(2,1)}, u32[]{:S(2)}) copy-start(bf16[4096,64]{0,1:T(8,128)(2,1)} %param.16) | copy-start | bytes 1572868
  0.9 7.6 %copy-start.5 = (s32[1,96]{1,0:T(1,128)S(1)}, s32[1,96]{1,0:T(1,128)}, u32[]{:S(2)}) copy-start(s32[1,96]{1,0:T(1,128)} %param.15) | copy-start | bytes 1156
  39.5 287.5 %all-to-all-start = ((f32[16,16,12288]{2,1,0:T(8,128)}), f32[16,16,12288]{2,1,0:T(8,128)}, u32[]{:S(2)}, u32[]{:S(2)}) async-start(f32[16,16,12288]{2,1,0:T(8,128)} %stack.2), calls=%async_computation | async-start | bytes 25165824 | tf_op jit(solution)/shard_map/all_to_all | solution.py:78
  358.2 1.0 copy-start.1
  374.8 7.0 %copy-start.2 = (f32[512,512]{1,0:T(8,128)S(1)}, f32[512,512]{1,0:T(8,128)}, u32[]{:S(2)}) copy-start(f32[512,512]{1,0:T(8,128)} %get-tuple-element.137) | copy-start | bytes 3145732 | tf_op jit(solution)/shard_map/while
  395.5 7.0 %copy-start.2 = (f32[512,512]{1,0:T(8,128)S(1)}, f32[512,512]{1,0:T(8,128)}, u32[]{:S(2)}) copy-start(f32[512,512]{1,0:T(8,128)} %get-tuple-element.137) | copy-start | bytes 3145732 | tf_op jit(solution)/shard_map/while
  416.2 7.0 %copy-start.2 = (f32[512,512]{1,0:T(8,128)S(1)}, f32[512,512]{1,0:T(8,128)}, u32[]{:S(2)}) copy-start(f32[512,512]{1,0:T(8,128)} %get-tuple-element.137) | copy-start | bytes 3145732 | tf_op jit(solution)/shard_map/while
  437.1 5.4 %copy-start.3 = (f32[512,512]{0,1:T(8,128)S(1)}, f32[512,512]{0,1:T(8,128)}, u32[]{:S(2)}) copy-start(f32[512,512]{0,1:T(8,128)} %get-tuple-element.44) | copy-start | bytes 3145732
